TPU v7x, 256 devices: a whole 4x4x8 slice. The times are simulated.
256 devices in a mesh: section: 4 (over x), ctx: 32 (over z, y), tp: 2 (over core).
Axes of the slice: x: 4, y: 4, z: 8, core: 2. Of those that a mesh axis runs over, the one named last changes fastest.
Arguments:
- hidden: bfloat16 [4, 4096, 8192], P('section', 'ctx', 'tp')
- gain: bfloat16 [4, 8192], P('section', 'tp'), may hold values from 0.5 to 1.5
- queries: bfloat16 [4, 4096, 32, 128], P('section', 'ctx', 'tp')
- key_value_weight: bfloat16 [4, 8192, 4, 2, 128], P('section', 'ctx', 'tp')
- adapt_down: bfloat16 [4, 16, 4096], P('section', None, 'tp'), may hold values from -1 to 1
- adapt_up: bfloat16 [4, 16, 8192], P('section', None, 'tp'), may hold values from -0.75 to 0.75
- out_grad: bfloat16 [4, 4096, 8192], P('section', 'ctx', 'tp'), may hold values from -6 to 6
- doc_ids: int32 [4096], P('ctx'), may hold values from 0 to 63, never falling along the last dimension, each value on 1 to 3072 neighbouring positions
Outputs:
- attention_out: bfloat16 [4, 4096, 4096], P('section', 'ctx', 'tp')
- adapter_out: bfloat16 [4, 4096, 8192], P('section', 'ctx', 'tp')
- grad_down: float32 [4, 16, 4096], P('section', None, 'tp')
- grad_up: float32 [4, 16, 8192], P('section', None, 'tp')
Inputs may be any that keep to these rules, and one draw needn't show every extreme that they name: doc_ids never falls along the sequence; a document spans at most three quarters of 4096 tokens, and one spans exactly that.
All inputs are finite; a program needn't handle non-finite values.
Results may differ from a plain program's by a relative error of at most 0.022.
Values may be sent and summed in bfloat16 or wider, within the bound.
A program may use at most 128 MiB of HBM per device.

v0:
```python
import math
import jax
import jax.numpy as jnp
from jax import lax
from jax.sharding import PartitionSpec as P


def rotate(head_values, positions):
    half_width = head_values.shape[-1] // 2
    freqs = 1000000.0 ** (-jnp.arange(half_width, dtype=jnp.float32) * 2.0 / head_values.shape[-1])
    angles = positions.astype(jnp.float32)[:, None] * freqs[None, :]
    cosine = jnp.cos(angles)[:, None, :]
    sine_table = jnp.sin(angles)[:, None, :]
    first_half = head_values[..., :half_width]
    second_half = head_values[..., half_width:]
    return jnp.concatenate(
        [
            first_half * cosine - second_half * sine_table,
            second_half * cosine + first_half * sine_table,
        ],
        axis=-1,
    )


def per_device(hidden, gain, queries, key_value_weight, adapt_down, adapt_up, out_grad, doc_ids):
    tp_count = lax.axis_size("tp")
    row_count = hidden.shape[1]
    local_width = hidden.shape[2]
    head_dim = key_value_weight.shape[-1]
    kv_count = key_value_weight.shape[2]
    head_count = queries.shape[2]
    group_size = head_count // kv_count
    local_query = head_count * head_dim
    rank_size = adapt_down.shape[1]
    key_block = 1024
    full_rows, full_gain = (
        lax.all_gather(hidden, "tp", axis=2, tiled=True),
        lax.all_gather(gain, "tp", axis=1, tiled=True),
    )
    widened = full_rows[0].astype(jnp.float32)
    normalized_rows = (
        widened
        * lax.rsqrt(jnp.mean(widened * widened, axis=1, keepdims=True) + 1e-06)
        * full_gain[0].astype(jnp.float32)
    ).astype(jnp.bfloat16)
    kv_local = key_value_weight.reshape(1, key_value_weight.shape[1], kv_count * 2 * head_dim)
    keyval_raw = jnp.dot(
        normalized_rows,
        lax.all_gather(kv_local, "ctx", axis=1, tiled=True)[0],
        preferred_element_type=jnp.float32,
    )
    positions = lax.axis_index("ctx") * row_count + jnp.arange(row_count, dtype=jnp.int32)
    key_value_rows = keyval_raw.reshape(row_count, kv_count, 2, head_dim)
    rotated_keys = rotate(key_value_rows[:, :, 0], positions).astype(jnp.bfloat16)
    value_rows = key_value_rows[:, :, 1].astype(jnp.bfloat16)
    rotated_query = rotate(queries[0].astype(jnp.float32), positions).astype(jnp.bfloat16)
    stacked = (
        rotated_query.reshape(row_count, kv_count, group_size, head_dim)
        .transpose(1, 2, 0, 3)
        .reshape(kv_count, group_size * row_count, head_dim)
    )
    query_pos = jnp.tile(positions, group_size)
    query_doc = jnp.tile(doc_ids, group_size).astype(jnp.float32)
    score_scale = head_dim ** (-0.5)
    start_state = (
        jnp.full((kv_count, group_size * row_count), -1e30, jnp.float32),
        jnp.zeros((kv_count, group_size * row_count), jnp.float32),
        jnp.zeros((kv_count, group_size * row_count, head_dim), jnp.float32),
    )
    carried = start_state
    first_row = jnp.int32(0)
    piece_keys = lax.all_gather(rotated_keys, "ctx", axis=0, tiled=True)
    piece_values = lax.all_gather(value_rows, "ctx", axis=0, tiled=True)
    piece_docs = lax.all_gather(doc_ids.astype(jnp.bfloat16), "ctx", axis=0, tiled=True)
    key_total = piece_keys.shape[0]
    for block_start in range(0, key_total, key_block):
        block_stop = min(key_total, block_start + key_block)
        block_keys = piece_keys[block_start:block_stop]
        block_values = piece_values[block_start:block_stop]
        key_pos = first_row + block_start + jnp.arange(block_keys.shape[0], dtype=jnp.int32)
        key_doc = piece_docs[block_start:block_stop].astype(jnp.float32)
        running_top, running_sum, running_acc = carried
        scores = (
            jnp.einsum("gqd,kgd->gqk", stacked, block_keys, preferred_element_type=jnp.float32)
            * score_scale
        )
        allowed = (
            (key_pos[None, :] <= query_pos[:, None]) & (key_doc[None, :] == query_doc[:, None])
        )[None]
        scores = jnp.where(allowed, scores, -1e30)
        new_top = jnp.maximum(running_top, jnp.max(scores, axis=2))
        weights = jnp.where(allowed, jnp.exp(scores - new_top[:, :, None]), 0.0)
        shrink = jnp.exp(running_top - new_top)
        new_acc = running_acc * shrink[:, :, None] + jnp.einsum(
            "gqk,kgd->gqd",
            weights.astype(jnp.bfloat16),
            block_values,
            preferred_element_type=jnp.float32,
        )
        carried = (new_top, running_sum * shrink + jnp.sum(weights, axis=2), new_acc)
    final_top, final_sum, final_acc = carried
    attended = (
        (final_acc / final_sum[:, :, None])
        .reshape(kv_count, group_size, row_count, head_dim)
        .transpose(2, 0, 1, 3)
        .reshape(row_count, local_query)
        .astype(jnp.bfloat16)
    )
    low_part = jnp.dot(attended, adapt_down[0].T, preferred_element_type=jnp.float32)
    back_part = jnp.dot(out_grad[0], adapt_up[0].T, preferred_element_type=jnp.float32)
    low_sum, back_sum = lax.psum((low_part, back_part), "tp")
    low_rows = low_sum.astype(jnp.bfloat16)
    back_rows = back_sum.astype(jnp.bfloat16)
    adapter_rows = jnp.dot(low_rows, adapt_up[0], preferred_element_type=jnp.float32).astype(
        jnp.bfloat16
    )
    up_part = jnp.dot(low_rows.T, out_grad[0], preferred_element_type=jnp.float32)
    down_part = jnp.dot(back_rows.T, attended, preferred_element_type=jnp.float32)
    ceiling = 0.5 * math.sqrt(
        lax.axis_size("section") * rank_size * (local_query + local_width) * tp_count
    )
    up_total, down_total = (
        lax.psum(up_part.astype(jnp.bfloat16), "ctx").astype(jnp.float32),
        lax.psum(down_part.astype(jnp.bfloat16), "ctx").astype(jnp.float32),
    )
    local_squares = jnp.sum(up_total * up_total) + jnp.sum(down_total * down_total)
    squares = lax.psum(local_squares, ("section", "tp"))
    factor = jnp.minimum(1.0, ceiling / (jnp.sqrt(squares) + 1e-06))
    grad_up = up_total * factor
    grad_down = down_total * factor
    return (attended[None], adapter_rows[None], grad_down[None], grad_up[None])


def solution(mesh):
    return jax.shard_map(
        per_device,
        mesh=mesh,
        in_specs=(
            P("section", "ctx", "tp"),
            P("section", "tp"),
            P("section", "ctx", "tp", None),
            P("section", "ctx", "tp", None, None),
            P("section", None, "tp"),
            P("section", None, "tp"),
            P("section", "ctx", "tp"),
            P("ctx"),
        ),
        out_specs=(
            P("section", "ctx", "tp"),
            P("section", "ctx", "tp"),
            P("section", None, "tp"),
            P("section", None, "tp"),
        ),
        check_vma=False,
    )
```

profile of v0, /device:TPU:1, one launch (start us, length us, event | category | flops | bytes accessed | tf_op | source)
XLA Modules:
  0.0 494.9 jit_solution(17314606590005313898)
XLA Ops:
  8.0 1.9 copy.81
  9.9 4.9 all_gather.20
  15.1 15.2 %all-gather.7.cloned.1.call-done = bf16[1,128,8192]{2,1,0:T(8,128)(2,1)} async-done(((bf16[1,128,4096]{2,1,0:T(8,128)(2,1)}), bf16[1,128,8192]{2,1,0:T(8,128)(2,1)}) %all-gather.7.cloned.1.call-update) | async-done | bytes 2097168 | tf_op jit(solution)/shard_map/all_gather | solution.py:37
  30.3 2.1 fusion.13
  32.4 102.8 %all-gather.9.cloned.1.call-done = bf16[1,8192,512]{1,2,0:T(8,128)(2,1)} async-done(((bf16[1,256,512]{1,2,0:T(8,128)(2,1)}), bf16[1,8192,512]{1,2,0:T(8,128)(2,1)}) %all-gather.9.cloned.1.call-update) | async-done | bytes 8388624 | tf_op jit(solution)/shard_map/all_gather | solution.py:49
  135.1 6.4 %fusion.30 = f32[128,2,2,128]{0,3,2,1:T(8,128)S(1)} fusion(bf16[2,2,128,8192]{3,2,1,0:T(8,128)(2,1)} %bitcast.101, bf16[1,128,8192]{2,1,0:T(8,128)(2,1)} %all-gather.7.cloned.1.call-done, f32[8192]{0:T(1024)S(1)} %bitcast.96, f32[128]{0:T(128)S(1)} %add_rsqrt_fusion), kind=kOutput, calls=%fused_computation.43 | convolution fusion | flops 1077936128 | bytes 10781184 | tf_op jit(solution)/shard_map/dot_general | solution.py:47
  143.5 28.6 %all-gather.1 = bf16[32,1,128]{2,1,0:T(2,128)(2,1)S(1)} all-gather(bf16[1,1,128]{2,1,0:T(2,128)(2,1)S(1)} %get-tuple-element.39), channel_id=1, replica_groups=mesh['section'=4,'ctx'=32,'tp'=2] {'ctx'}, dimensions={0}, use_global_device_ids=true | all-gather | bytes 8448 | tf_op jit(solution)/shard_map/all_gather | solution.py:74
  172.2 1.1 pad_maximum_fusion
  173.7 4.4 fusion.24
  179.1 35.1 %all-gather.11.cloned.1.call-done = bf16[4096,2,128]{0,2,1:T(8,128)(2,1)} async-done(((bf16[128,2,128]{0,2,1:T(8,128)(2,1)}), bf16[4096,2,128]{0,2,1:T(8,128)(2,1)}) %all-gather.11.cloned.1.call-update) | async-done | bytes 2097168 | tf_op jit(solution)/shard_map/all_gather | solution.py:72
  214.2 3.3 fusion
  217.6 2.2 fusion.2
  219.8 5.8 %fusion.1 = (f32[2,1024]{1,0:T(2,128)S(1)}, f32[2,1024,1024]{1,2,0:T(8,128)}) fusion(pred[1024,1024]{0,1:T(8,128)(4,1)S(1)} %copy-done.9, bf16[2,1024,128]{2,1,0:T(8,128)(2,1)S(1)} %bitcast.93, bf16[4096,2,128]{0,2,1:T(8,128)(2,1)S(1)} %copy-done.15), kind=kOutput, calls=%fused_computation.9 | convolution fusion | flops 543160320 | bytes 10493952 | tf_op jit(solution)/shard_map/gqd,kgd->gqk/dot_general | solution.py:84
  225.6 2.2 fusion.3
  227.8 9.7 %fusion.4 = (f32[2,1024]{1,0:T(2,128)S(1)}, f32[2,1024]{1,0:T(2,128)S(1)}) fusion(f32[2,1024,1024]{1,2,0:T(8,128)S(1)} %get-tuple-element.48, f32[2,1024]{1,0:T(2,128)S(1)} %get-tuple-element.32, pred[1024,1024]{0,1:T(8,128)(4,1)S(1)} %get-tuple-element.33, f32[2,1024]{1,0:T(2,128)S(1)} %get-tuple-element.22, f32[2,1024,1024]{1,2,0:T(8,128)} %get-tuple-element.46, ...), kind=kLoop, calls=%fused_computation.12 | loop fusion | flops 20967424 | bytes 18907136 | tf_op jit(solution)/shard_map/reduce_sum | solution.py:100
  237.6 5.8 %fusion.8 = (f32[2,1024]{1,0:T(2,128)S(1)}, f32[2,1024]{1,0:T(2,128)S(1)}) fusion(f32[2,1024,1024]{1,2,0:T(8,128)S(1)} %get-tuple-element.44, f32[2,1024]{1,0:T(2,128)S(1)} %get-tuple-element.21, pred[1024,1024]{0,1:T(8,128)(4,1)} %get-tuple-element.35, f32[2,1024]{1,0:T(2,128)S(1)} %get-tuple-element.20, f32[2,1024,1024]{1,2,0:T(8,128)S(1)} %get-tuple-element.42, ...), kind=kLoop, calls=%fused_computation.16 | loop fusion | flops 20967424 | bytes 18907136 | tf_op jit(solution)/shard_map/reduce_sum | solution.py:100
  243.5 47.7 %all-gather.13.cloned.1.call-done = bf16[4096,2,1,128]{0,3,2,1:T(8,128)(2,1)} async-done(((bf16[128,2,1,128]{0,3,2,1:T(8,128)(2,1)}), bf16[4096,2,1,128]{0,3,2,1:T(8,128)(2,1)}) %all-gather.13.cloned.1.call-update) | async-done | bytes 2097168 | tf_op jit(solution)/shard_map/all_gather | solution.py:73
  291.2 7.9 %fusion.20 = f32[2,1024,128]{2,1,0:T(8,128)} fusion(f32[2,1024,1024]{1,2,0:T(8,128)} %get-tuple-element.46, f32[2,1024]{1,0:T(2,128)S(1)} %get-tuple-element.22, pred[1024,1024]{0,1:T(8,128)(4,1)S(1)} %copy-done.10, bf16[4096,2,1,128]{0,3,2,1:T(8,128)(2,1)} %all-gather.13.cloned.1.call-done), kind=kOutput, calls=%fused_computation.31 | convolution fusion | flops 547356672 | bytes 11018240 | tf_op jit(solution)/shard_map/gqk,kgd->gqd/dot_general | solution.py:94
  299.0 5.6 %fusion.18 = f32[2,1024,128]{2,1,0:T(8,128)} fusion(f32[2,1024,1024]{1,2,0:T(8,128)S(1)} %copy-done.3, f32[2,1024]{1,0:T(2,128)S(1)} %get-tuple-element.21, pred[1024,1024]{0,1:T(8,128)(4,1)} %get-tuple-element.35, bf16[4096,2,1,128]{0,3,2,1:T(8,128)(2,1)} %all-gather.13.cloned.1.call-done), kind=kOutput, calls=%fused_computation.30 | convolution fusion | flops 547356672 | bytes 11018240 | tf_op jit(solution)/shard_map/gqk,kgd->gqd/dot_general | solution.py:94
  304.7 4.9 fusion.16
  309.7 5.5 %divide_convert_fusion = bf16[2,1024,128]{2,1,0:T(8,128)(2,1)S(1)} fusion(f32[2,1024,128]{2,1,0:T(8,128)S(1)} %fusion.16, f32[2,1024,128]{2,1,0:T(8,128)S(1)} %copy-done.18, f32[2,1024,128]{2,1,0:T(8,128)S(1)} %copy-done.17, f32[2,1024,1024]{1,2,0:T(8,128)S(1)} %bitcast.84, f32[2,1024]{1,0:T(2,128)S(1)} %get-tuple-element.32, ...), kind=kOutput, calls=%fused_computation.56 | convolution fusion | flops 549715968 | bytes 13680640 | tf_op jit(solution)/shard_map/gqk,kgd->gqd/dot_general | solution.py:94
  315.7 6.8 %all-reduce = (bf16[128,16]{0,1:T(8,128)(2,1)S(1)}, bf16[128,16]{0,1:T(8,128)(2,1)S(1)}) all-reduce(f32[128,16]{0,1:T(8,128)S(1)} %fusion.76, f32[128,16]{0,1:T(8,128)S(1)} %fusion.56), channel_id=1, replica_groups=mesh['section'=4,'ctx'=32,'tp'=2] {'tp'}, use_global_device_ids=true, to_apply=%region_9.10 | all-reduce | flops 4096 | bytes 24576 | tf_op jit(solution)/shard_map/psum | solution.py:111
  322.5 0.9 convolution_convert_fusion.2
  323.4 0.9 convolution_convert_fusion.1
  324.3 1.4 fusion.12
  325.8 135.9 %all-reduce.4.cloned.1.call-done = (bf16[16,2048]{1,0:T(8,128)(2,1)}, bf16[16,4096]{1,0:T(8,128)(2,1)}) async-done(((bf16[16,2048]{1,0:T(8,128)(2,1)}, bf16[16,4096]{1,0:T(8,128)(2,1)}), (bf16[16,2048]{1,0:T(8,128)(2,1)}, bf16[16,4096]{1,0:T(8,128)(2,1)})) %all-reduce.4.cloned.1.call-update) | async-done | bytes 196624 | tf_op jit(solution)/shard_map/psum | solution.py:124
  461.7 1.6 fusion.70
  463.3 1.5 fusion.72
  466.0 1.0 copy.67
  467.1 17.5 %psum.39 = f32[]{:T(128)} all-reduce(f32[]{:T(128)S(6)} %add.137), channel_id=1, replica_groups=mesh['section'=4,'ctx'=32,'tp'=2] {'section','tp'}, use_global_device_ids=true, to_apply=%region_15.16 | all-reduce | flops 1 | bytes 8 | tf_op jit(solution)/shard_map/psum | solution.py:127
  485.2 1.6 fusion.71
  486.9 1.5 fusion.73
  (86 shorter events, 4.9 us)
Async XLA Ops:
  7.2 166.1 %copy-start = (bf16[1,128,4096]{2,1,0:T(8,128)(2,1)S(1)}, bf16[1,128,4096]{2,1,0:T(8,128)(2,1)}, u32[]{:S(2)}) copy-start(bf16[1,128,4096]{2,1,0:T(8,128)(2,1)} %param.14) | copy-start | bytes 3145732
  7.2 23.1 %all-gather.7.cloned.1.call-start = ((), (), s32[]{:S(2)}) async-start(), calls=%async_computation | async-start | bytes 3145728 | tf_op jit(solution)/shard_map/all_gather | solution.py:37
  7.9 134.6 %copy-start.11 = (bf16[1,128,16,128]{3,2,1,0:T(8,128)(2,1)S(1)}, bf16[1,128,16,128]{3,2,1,0:T(8,128)(2,1)}, u32[]{:S(2)}) copy-start(bf16[1,128,16,128]{3,2,1,0:T(8,128)(2,1)} %param.10) | copy-start | bytes 1572868
  7.9 127.2 %all-gather.9.cloned.1.call-start = ((), (), s32[]{:S(2)}) async-start(), calls=%async_computation.1 | async-start | bytes 8650752 | tf_op jit(solution)/shard_map/all_gather | solution.py:49
  9.9 204.3 %all-gather.11.cloned.1.call-start = ((), (), s32[]{:S(2)}) async-start(), calls=%async_computation.2 | async-start | bytes 2162688 | tf_op jit(solution)/shard_map/all_gather | solution.py:72
  135.1 8.3 %copy-start.16 = (s32[128]{0:T(128)S(1)}, s32[128]{0:T(128)}, u32[]{:S(2)}) copy-start(s32[128]{0:T(128)} %param.15) | copy-start | bytes 1540
  135.1 38.2 %copy-start.13 = (bf16[1,16,4096]{2,1,0:T(8,128)(2,1)S(1)}, bf16[1,16,4096]{2,1,0:T(8,128)(2,1)}, u32[]{:S(2)}) copy-start(bf16[1,16,4096]{2,1,0:T(8,128)(2,1)} %param.13) | copy-start | bytes 393220
  142.3 148.8 %all-gather.13.cloned.1.call-start = ((), (), s32[]{:S(2)}) async-start(), calls=%async_computation.3 | async-start | bytes 2162688 | tf_op jit(solution)/shard_map/all_gather | solution.py:73
  178.1 49.7 %copy-start.5 = (pred[1024,1024]{0,1:T(8,128)(4,1)}, pred[1024,1024]{0,1:T(8,128)(4,1)S(1)}, u32[]{:S(2)}) copy-start(pred[1024,1024]{0,1:T(8,128)(4,1)S(1)} %get-tuple-element.33) | copy-start | bytes 3145732
  178.1 59.5 %copy-start.7 = (pred[1024,1024]{0,1:T(8,128)(4,1)}, pred[1024,1024]{0,1:T(8,128)(4,1)S(1)}, u32[]{:S(2)}) copy-start(pred[1024,1024]{0,1:T(8,128)(4,1)S(1)} %get-tuple-element.36) | copy-start | bytes 3145732
  178.8 282.9 %all-reduce.4.cloned.1.call-start = ((), (), s32[]{:S(2)}) async-start(), calls=%async_computation.4 | async-start | bytes 393216 | tf_op jit(solution)/shard_map/psum | solution.py:124
  214.2 3.3 copy-start.8
  214.2 3.4 copy-start.12
  214.2 3.4 copy-start.15
  217.5 10.3 %copy-start.1 = (f32[2,1024,1024]{1,2,0:T(8,128)}, f32[2,1024,1024]{1,2,0:T(8,128)S(1)}, u32[]{:S(2)}) copy-start(f32[2,1024,1024]{1,2,0:T(8,128)S(1)} %get-tuple-element.48) | copy-start | bytes 25165828
  217.5 2.2 copy-start.9
  219.7 17.9 %copy-start.2 = (f32[2,1024,1024]{1,2,0:T(8,128)}, f32[2,1024,1024]{1,2,0:T(8,128)S(1)}, u32[]{:S(2)}) copy-start(f32[2,1024,1024]{1,2,0:T(8,128)S(1)} %get-tuple-element.44) | copy-start | bytes 25165828
  227.8 9.8 %copy-start.4 = (f32[2,1024,1024]{1,2,0:T(8,128)}, f32[2,1024,1024]{1,2,0:T(8,128)S(1)}, u32[]{:S(2)}) copy-start(f32[2,1024,1024]{1,2,0:T(8,128)S(1)} %get-tuple-element.42) | copy-start | bytes 25165828
  237.6 53.5 %copy-start.10 = (pred[1024,1024]{0,1:T(8,128)(4,1)S(1)}, pred[1024,1024]{0,1:T(8,128)(4,1)}, u32[]{:S(2)}) copy-start(pred[1024,1024]{0,1:T(8,128)(4,1)} %get-tuple-element.34) | copy-start | bytes 3145732
  291.2 7.9 %copy-start.3 = (f32[2,1024,1024]{1,2,0:T(8,128)S(1)}, f32[2,1024,1024]{1,2,0:T(8,128)}, u32[]{:S(2)}) copy-start(f32[2,1024,1024]{1,2,0:T(8,128)} %copy-done.2) | copy-start | bytes 25165828
  291.2 13.5 %slice-start.2 = ((s8[8388608]{0:T(1024)(128)(4,1)}), s8[4194304]{0:T(1024)(128)(4,1)S(1)}, s32[]{:S(2)}) async-start(s8[8388608]{0:T(1024)(128)(4,1)} %bitcast.85), calls=%async_computation.7 | async-start | bytes 8388608
  299.0 5.6 %slice-start.3 = ((s8[8388608]{0:T(1024)(128)(4,1)}), s8[4194304]{0:T(1024)(128)(4,1)S(1)}, s32[]{:S(2)}) async-start(s8[8388608]{0:T(1024)(128)(4,1)} %bitcast.85), calls=%async_computation.8 | async-start | bytes 8388608
  299.0 10.6 %slice-start = ((s8[8388608]{0:T(1024)(128)(4,1)}), s8[4194304]{0:T(1024)(128)(4,1)S(1)}, s32[]{:S(2)}) async-start(s8[8388608]{0:T(1024)(128)(4,1)} %bitcast.83), calls=%async_computation.5 | async-start | bytes 8388608
  304.7 5.0 %slice-start.1 = ((s8[8388608]{0:T(1024)(128)(4,1)}), s8[4194304]{0:T(1024)(128)(4,1)S(1)}, s32[]{:S(2)}) async-start(s8[8388608]{0:T(1024)(128)(4,1)} %bitcast.83), calls=%async_computation.6 | async-start | bytes 8388608
  304.7 5.0 %copy-start.6 = (pred[1024,1024]{0,1:T(8,128)(4,1)S(1)}, pred[1024,1024]{0,1:T(8,128)(4,1)}, u32[]{:S(2)}) copy-start(pred[1024,1024]{0,1:T(8,128)(4,1)} %copy-done.5) | copy-start | bytes 3145732
  304.7 5.0 %copy-start.17 = (f32[2,1024,128]{2,1,0:T(8,128)S(1)}, f32[2,1024,128]{2,1,0:T(8,128)}, u32[]{:S(2)}) copy-start(f32[2,1024,128]{2,1,0:T(8,128)} %fusion.20) | copy-start | bytes 3145732
  304.7 5.0 %copy-start.18 = (f32[2,1024,128]{2,1,0:T(8,128)S(1)}, f32[2,1024,128]{2,1,0:T(8,128)}, u32[]{:S(2)}) copy-start(f32[2,1024,128]{2,1,0:T(8,128)} %fusion.18) | copy-start | bytes 3145732
  309.7 5.8 %copy-start.14 = (bf16[1,16,2048]{2,1,0:T(8,128)(2,1)S(1)}, bf16[1,16,2048]{2,1,0:T(8,128)(2,1)}, u32[]{:S(2)}) copy-start(bf16[1,16,2048]{2,1,0:T(8,128)(2,1)} %param.12) | copy-start | bytes 196612
Sparse Core Ops, SparseCore 0:
  9.8 20.4 all-gather.6
  33.3 101.7 all-gather.8
  142.4 71.7 all-gather.10
  217.1 74.0 all-gather.12
  324.5 137.1 all-reduce.3
where the time goes:
time: 495 us
  waiting for transfers between devices  337 us (68%)
  blocking collectives  57.8 us (12%)
  matrix products  47.6 us (10%)
  other arithmetic  31 us (6%)
  between operations  16.3 us (3%)
    psum x1, waiting for transfers between devices, per_device(): lax.psum(down_part.astype(jnp.bfloat16), 'ctx').astype(jnp.float32)  136 us
    all_gather x1, waiting for transfers between devices, per_device(): lax.all_gather(kv_local, 'ctx', axis=1, tiled=True)[0]  103 us
    all_gather x1, waiting for transfers between devices, per_device(): piece_values = lax.all_gather(value_rows, 'ctx', axis=0, tiled=True)  47.7 us
    all_gather x1, waiting for transfers between devices, per_device(): piece_keys = lax.all_gather(rotated_keys, 'ctx', axis=0, tiled=True)  35.1 us
    all_gather x1, blocking collectives, per_device(): lax.all_gather(doc_ids.astype(jnp.bfloat16), 'ctx', axis=0, tiled=True)  28.6 us
    dot_general x4, matrix products, per_device(): jnp.einsum('gqk,kgd->gqd', weights.astype(jnp.bfloat16), block_values, pr...  23.9 us
    psum x1, blocking collectives, per_device(): squares = lax.psum(local_squares, ('section', 'tp'))  17.5 us
    reduce_sum x2, other arithmetic, per_device(): jnp.sum(weights, axis=2)  15.6 us
  transfers between devices with their start and end apart: 5, of which 5 were waited for; matrix products, arithmetic and copies ran while one was open for 9% of the time, Pallas kernels for 0%

commit v1 on v0

--- a/solution.py
+++ b/solution.py
@@ -121,7 +121,7 @@
     )
     up_total, down_total = (
         lax.psum(up_part.astype(jnp.bfloat16), "ctx").astype(jnp.float32),
-        lax.psum(down_part.astype(jnp.bfloat16), "ctx").astype(jnp.float32),
+        jnp.sum(lax.all_gather(down_part.astype(jnp.bfloat16), "ctx"), axis=0).astype(jnp.float32),
     )
     local_squares = jnp.sum(up_total * up_total) + jnp.sum(down_total * down_total)
     squares = lax.psum(local_squares, ("section", "tp"))

time: 495 us -> 571 us (1.15)
  waiting for transfers between devices: 337 us -> 413 us
    all_gather x0 -> x1, waiting for transfers between devices: none -> 77.9 us  [per_device(): lax.all_gather(down_part.astype(jnp.bfloat16), 'ctx')]
  transfers between devices with their start and end apart: 5 -> 6, of which waited for: 5 -> 6; matrix products, arithmetic and copies ran while one was open for 9% -> 8% of each run, Pallas kernels for 0% -> 0%
where the time goes in v1:
time: 571 us
  waiting for transfers between devices  413 us (72%)
  blocking collectives  57.2 us (10%)
  matrix products  47.6 us (8%)
  other arithmetic  31.2 us (5%)
  between operations  16.6 us (3%)
    psum x1, waiting for transfers between devices, per_device(): lax.psum(up_part.astype(jnp.bfloat16), 'ctx').astype(jnp.float32)  134 us
    all_gather x1, waiting for transfers between devices, per_device(): lax.all_gather(kv_local, 'ctx', axis=1, tiled=True)[0]  103 us
    all_gather x1, waiting for transfers between devices, per_device(): lax.all_gather(down_part.astype(jnp.bfloat16), 'ctx')  77.9 us
    all_gather x1, waiting for transfers between devices, per_device(): piece_values = lax.all_gather(value_rows, 'ctx', axis=0, tiled=True)  47.7 us
    all_gather x1, waiting for transfers between devices, per_device(): piece_keys = lax.all_gather(rotated_keys, 'ctx', axis=0, tiled=True)  35.1 us
    all_gather x1, blocking collectives, per_device(): lax.all_gather(doc_ids.astype(jnp.bfloat16), 'ctx', axis=0, tiled=True)  28.6 us
    dot_general x4, matrix products, per_device(): jnp.einsum('gqk,kgd->gqd', weights.astype(jnp.bfloat16), block_values, pr...  23.9 us
    psum x1, blocking collectives, per_device(): squares = lax.psum(local_squares, ('section', 'tp'))  16.8 us
  transfers between devices with their start and end apart: 6, of which 6 were waited for; matrix products, arithmetic and copies ran while one was open for 8% of the time, Pallas kernels for 0%

profile of v1, /device:TPU:1, one launch (start us, length us, event | category | flops | bytes accessed | tf_op | source)
XLA Modules:
  0.0 570.5 jit_solution(13645098928092295871)
XLA Ops:
  8.0 1.9 copy.81
  9.9 4.9 all_gather.26
  15.1 15.2 %all-gather.9.cloned.1.call-done = bf16[1,128,8192]{2,1,0:T(8,128)(2,1)} async-done(((bf16[1,128,4096]{2,1,0:T(8,128)(2,1)}), bf16[1,128,8192]{2,1,0:T(8,128)(2,1)}) %all-gather.9.cloned.1.call-update) | async-done | bytes 2097168 | tf_op jit(solution)/shard_map/all_gather | solution.py:37
  30.3 2.1 fusion.13
  32.4 102.8 %all-gather.11.cloned.1.call-done = bf16[1,8192,512]{1,2,0:T(8,128)(2,1)} async-done(((bf16[1,256,512]{1,2,0:T(8,128)(2,1)}), bf16[1,8192,512]{1,2,0:T(8,128)(2,1)}) %all-gather.11.cloned.1.call-update) | async-done | bytes 8388624 | tf_op jit(solution)/shard_map/all_gather | solution.py:49
  135.1 6.4 %fusion.30 = f32[128,2,2,128]{0,3,2,1:T(8,128)S(1)} fusion(bf16[2,2,128,8192]{3,2,1,0:T(8,128)(2,1)} %bitcast.103, bf16[1,128,8192]{2,1,0:T(8,128)(2,1)} %all-gather.9.cloned.1.call-done, f32[8192]{0:T(1024)S(1)} %bitcast.98, f32[128]{0:T(128)S(1)} %add_rsqrt_fusion), kind=kOutput, calls=%fused_computation.43 | convolution fusion | flops 1077936128 | bytes 10781184 | tf_op jit(solution)/shard_map/dot_general | solution.py:47
  143.5 28.6 %all-gather.2 = bf16[32,1,128]{2,1,0:T(2,128)(2,1)S(1)} all-gather(bf16[1,1,128]{2,1,0:T(2,128)(2,1)S(1)} %get-tuple-element.37), channel_id=1, replica_groups=mesh['section'=4,'ctx'=32,'tp'=2] {'ctx'}, dimensions={0}, use_global_device_ids=true | all-gather | bytes 8448 | tf_op jit(solution)/shard_map/all_gather | solution.py:74
  172.2 1.1 pad_maximum_fusion
  173.7 4.4 fusion.24
  179.0 35.1 %all-gather.13.cloned.1.call-done = bf16[4096,2,128]{0,2,1:T(8,128)(2,1)} async-done(((bf16[128,2,128]{0,2,1:T(8,128)(2,1)}), bf16[4096,2,128]{0,2,1:T(8,128)(2,1)}) %all-gather.13.cloned.1.call-update) | async-done | bytes 2097168 | tf_op jit(solution)/shard_map/all_gather | solution.py:72
  214.2 3.3 fusion
  217.6 2.2 fusion.2
  219.8 5.8 %fusion.1 = (f32[2,1024]{1,0:T(2,128)S(1)}, f32[2,1024,1024]{1,2,0:T(8,128)}) fusion(pred[1024,1024]{0,1:T(8,128)(4,1)S(1)} %copy-done.9, bf16[2,1024,128]{2,1,0:T(8,128)(2,1)S(1)} %bitcast.95, bf16[4096,2,128]{0,2,1:T(8,128)(2,1)S(1)} %copy-done.15), kind=kOutput, calls=%fused_computation.9 | convolution fusion | flops 543160320 | bytes 10493952 | tf_op jit(solution)/shard_map/gqd,kgd->gqk/dot_general | solution.py:84
  225.6 2.2 fusion.3
  227.8 9.7 %fusion.4 = (f32[2,1024]{1,0:T(2,128)S(1)}, f32[2,1024]{1,0:T(2,128)S(1)}) fusion(f32[2,1024,1024]{1,2,0:T(8,128)S(1)} %get-tuple-element.46, f32[2,1024]{1,0:T(2,128)S(1)} %get-tuple-element.30, pred[1024,1024]{0,1:T(8,128)(4,1)S(1)} %get-tuple-element.31, f32[2,1024]{1,0:T(2,128)S(1)} %get-tuple-element.20, f32[2,1024,1024]{1,2,0:T(8,128)} %get-tuple-element.44, ...), kind=kLoop, calls=%fused_computation.12 | loop fusion | flops 20967424 | bytes 18907136 | tf_op jit(solution)/shard_map/reduce_sum | solution.py:100
  237.6 5.8 %fusion.8 = (f32[2,1024]{1,0:T(2,128)S(1)}, f32[2,1024]{1,0:T(2,128)S(1)}) fusion(f32[2,1024,1024]{1,2,0:T(8,128)S(1)} %get-tuple-element.42, f32[2,1024]{1,0:T(2,128)S(1)} %get-tuple-element.19, pred[1024,1024]{0,1:T(8,128)(4,1)} %get-tuple-element.33, f32[2,1024]{1,0:T(2,128)S(1)} %get-tuple-element.18, f32[2,1024,1024]{1,2,0:T(8,128)S(1)} %get-tuple-element.40, ...), kind=kLoop, calls=%fused_computation.16 | loop fusion | flops 20967424 | bytes 18907136 | tf_op jit(solution)/shard_map/reduce_sum | solution.py:100
  243.5 47.7 %all-gather.15.cloned.1.call-done = bf16[4096,2,1,128]{0,3,2,1:T(8,128)(2,1)} async-done(((bf16[128,2,1,128]{0,3,2,1:T(8,128)(2,1)}), bf16[4096,2,1,128]{0,3,2,1:T(8,128)(2,1)}) %all-gather.15.cloned.1.call-update) | async-done | bytes 2097168 | tf_op jit(solution)/shard_map/all_gather | solution.py:73
  291.2 7.9 %fusion.20 = f32[2,1024,128]{2,1,0:T(8,128)} fusion(f32[2,1024,1024]{1,2,0:T(8,128)} %get-tuple-element.44, f32[2,1024]{1,0:T(2,128)S(1)} %get-tuple-element.20, pred[1024,1024]{0,1:T(8,128)(4,1)S(1)} %copy-done.10, bf16[4096,2,1,128]{0,3,2,1:T(8,128)(2,1)} %all-gather.15.cloned.1.call-done), kind=kOutput, calls=%fused_computation.31 | convolution fusion | flops 547356672 | bytes 11018240 | tf_op jit(solution)/shard_map/gqk,kgd->gqd/dot_general | solution.py:94
  299.0 5.6 fusion.18
  304.7 4.9 fusion.16
  309.7 5.5 divide_convert_fusion
  315.7 6.8 %all-reduce = (bf16[128,16]{0,1:T(8,128)(2,1)S(1)}, bf16[128,16]{0,1:T(8,128)(2,1)S(1)}) all-reduce(f32[128,16]{0,1:T(8,128)S(1)} %fusion.76, f32[128,16]{0,1:T(8,128)S(1)} %fusion.56), channel_id=1, replica_groups=mesh['section'=4,'ctx'=32,'tp'=2] {'tp'}, use_global_device_ids=true, to_apply=%region_9.10 | all-reduce | flops 4096 | bytes 24576 | tf_op jit(solution)/shard_map/psum | solution.py:111
  322.5 0.9 convolution_convert_fusion.1
  323.5 0.9 convolution_convert_fusion.2
  324.4 1.4 fusion.12
  325.8 133.7 %all-reduce.3.cloned.1.call-done = bf16[16,4096]{1,0:T(8,128)(2,1)} async-done(((bf16[16,4096]{1,0:T(8,128)(2,1)}), bf16[16,4096]{1,0:T(8,128)(2,1)}) %all-reduce.3.cloned.1.call-update) | async-done | bytes 131088 | tf_op jit(solution)/shard_map/psum | solution.py:123
  459.5 1.6 fusion.70
  461.1 77.9 %all-gather.17.cloned.1.call-done = bf16[512,2048]{1,0:T(8,128)(2,1)} async-done(((bf16[16,2048]{1,0:T(8,128)(2,1)}), bf16[512,2048]{1,0:T(8,128)(2,1)}) %all-gather.17.cloned.1.call-update) | async-done | bytes 2097168 | tf_op jit(solution)/shard_map/all_gather | solution.py:124
  539.0 1.9 reduce_sum.80
  542.8 1.0 copy.67
  543.8 16.8 %psum.31 = f32[]{:T(128)} all-reduce(f32[]{:T(128)S(6)} %add.135), channel_id=1, replica_groups=mesh['section'=4,'ctx'=32,'tp'=2] {'section','tp'}, use_global_device_ids=true, to_apply=%region_15.16 | all-reduce | flops 1 | bytes 8 | tf_op jit(solution)/shard_map/psum | solution.py:127
  562.0 1.6 fusion.71
  (90 shorter events, 6.2 us)
Async XLA Ops:
  7.2 166.1 %copy-start = (bf16[1,128,4096]{2,1,0:T(8,128)(2,1)S(1)}, bf16[1,128,4096]{2,1,0:T(8,128)(2,1)}, u32[]{:S(2)}) copy-start(bf16[1,128,4096]{2,1,0:T(8,128)(2,1)} %param.14) | copy-start | bytes 3145732
  7.2 23.1 %all-gather.9.cloned.1.call-start = ((), (), s32[]{:S(2)}) async-start(), calls=%async_computation | async-start | bytes 3145728 | tf_op jit(solution)/shard_map/all_gather | solution.py:37
  7.9 134.6 %copy-start.11 = (bf16[1,128,16,128]{3,2,1,0:T(8,128)(2,1)S(1)}, bf16[1,128,16,128]{3,2,1,0:T(8,128)(2,1)}, u32[]{:S(2)}) copy-start(bf16[1,128,16,128]{3,2,1,0:T(8,128)(2,1)} %param.10) | copy-start | bytes 1572868
  7.9 127.2 %all-gather.11.cloned.1.call-start = ((), (), s32[]{:S(2)}) async-start(), calls=%async_computation.1 | async-start | bytes 8650752 | tf_op jit(solution)/shard_map/all_gather | solution.py:49
  9.9 204.3 %all-gather.13.cloned.1.call-start = ((), (), s32[]{:S(2)}) async-start(), calls=%async_computation.2 | async-start | bytes 2162688 | tf_op jit(solution)/shard_map/all_gather | solution.py:72
  135.1 8.3 %copy-start.16 = (s32[128]{0:T(128)S(1)}, s32[128]{0:T(128)}, u32[]{:S(2)}) copy-start(s32[128]{0:T(128)} %param.15) | copy-start | bytes 1540
  135.1 38.2 %copy-start.13 = (bf16[1,16,4096]{2,1,0:T(8,128)(2,1)S(1)}, bf16[1,16,4096]{2,1,0:T(8,128)(2,1)}, u32[]{:S(2)}) copy-start(bf16[1,16,4096]{2,1,0:T(8,128)(2,1)} %param.13) | copy-start | bytes 393220
  142.3 148.8 %all-gather.15.cloned.1.call-start = ((), (), s32[]{:S(2)}) async-start(), calls=%async_computation.4 | async-start | bytes 2162688 | tf_op jit(solution)/shard_map/all_gather | solution.py:73
  178.1 49.7 %copy-start.5 = (pred[1024,1024]{0,1:T(8,128)(4,1)}, pred[1024,1024]{0,1:T(8,128)(4,1)S(1)}, u32[]{:S(2)}) copy-start(pred[1024,1024]{0,1:T(8,128)(4,1)S(1)} %get-tuple-element.31) | copy-start | bytes 3145732
  178.1 59.5 %copy-start.7 = (pred[1024,1024]{0,1:T(8,128)(4,1)}, pred[1024,1024]{0,1:T(8,128)(4,1)S(1)}, u32[]{:S(2)}) copy-start(pred[1024,1024]{0,1:T(8,128)(4,1)S(1)} %get-tuple-element.34) | copy-start | bytes 3145732
  178.8 280.7 %all-reduce.3.cloned.1.call-start = ((), (), s32[]{:S(2)}) async-start(), calls=%async_computation.3 | async-start | bytes 262144 | tf_op jit(solution)/shard_map/psum | solution.py:123
  214.2 3.3 copy-start.8
  214.2 3.4 copy-start.12
  214.2 3.4 copy-start.15
  217.5 10.3 %copy-start.1 = (f32[2,1024,1024]{1,2,0:T(8,128)}, f32[2,1024,1024]{1,2,0:T(8,128)S(1)}, u32[]{:S(2)}) copy-start(f32[2,1024,1024]{1,2,0:T(8,128)S(1)} %get-tuple-element.46) | copy-start | bytes 25165828
  217.5 2.2 copy-start.9
  219.7 17.8 %copy-start.2 = (f32[2,1024,1024]{1,2,0:T(8,128)}, f32[2,1024,1024]{1,2,0:T(8,128)S(1)}, u32[]{:S(2)}) copy-start(f32[2,1024,1024]{1,2,0:T(8,128)S(1)} %get-tuple-element.42) | copy-start | bytes 25165828
  227.8 9.8 %copy-start.4 = (f32[2,1024,1024]{1,2,0:T(8,128)}, f32[2,1024,1024]{1,2,0:T(8,128)S(1)}, u32[]{:S(2)}) copy-start(f32[2,1024,1024]{1,2,0:T(8,128)S(1)} %get-tuple-element.40) | copy-start | bytes 25165828
  237.6 53.6 %copy-start.10 = (pred[1024,1024]{0,1:T(8,128)(4,1)S(1)}, pred[1024,1024]{0,1:T(8,128)(4,1)}, u32[]{:S(2)}) copy-start(pred[1024,1024]{0,1:T(8,128)(4,1)} %get-tuple-element.32) | copy-start | bytes 3145732
  291.2 7.9 %copy-start.3 = (f32[2,1024,1024]{1,2,0:T(8,128)S(1)}, f32[2,1024,1024]{1,2,0:T(8,128)}, u32[]{:S(2)}) copy-start(f32[2,1024,1024]{1,2,0:T(8,128)} %copy-done.2) | copy-start | bytes 25165828
  291.2 13.5 %slice-start.2 = ((s8[8388608]{0:T(1024)(128)(4,1)}), s8[4194304]{0:T(1024)(128)(4,1)S(1)}, s32[]{:S(2)}) async-start(s8[8388608]{0:T(1024)(128)(4,1)} %bitcast.86), calls=%async_computation.8 | async-start | bytes 8388608
  299.0 5.6 slice-start.3
  299.0 10.6 %slice-start = ((s8[8388608]{0:T(1024)(128)(4,1)}), s8[4194304]{0:T(1024)(128)(4,1)S(1)}, s32[]{:S(2)}) async-start(s8[8388608]{0:T(1024)(128)(4,1)} %bitcast.84), calls=%async_computation.6 | async-start | bytes 8388608
  304.7 5.0 slice-start.1
  304.7 5.0 copy-start.6
  304.7 5.0 copy-start.17
  304.7 5.0 copy-start.18
  309.7 5.8 %copy-start.14 = (bf16[1,16,2048]{2,1,0:T(8,128)(2,1)S(1)}, bf16[1,16,2048]{2,1,0:T(8,128)(2,1)}, u32[]{:S(2)}) copy-start(bf16[1,16,2048]{2,1,0:T(8,128)(2,1)} %param.12) | copy-start | bytes 196612
  323.4 215.5 %all-gather.17.cloned.1.call-start = ((), (), s32[]{:S(2)}) async-start(), calls=%async_computation.5 | async-start | bytes 2162688 | tf_op jit(solution)/shard_map/all_gather | solution.py:124
Sparse Core Ops, SparseCore 0:
  9.8 20.4 all-gather.8
  33.3 101.7 all-gather.10
  142.4 71.7 all-gather.12
  217.1 74.0 all-gather.14
  323.6 135.8 all-reduce.2
  462.8 76.0 all-gather.16
